TPU v7x, 32 devices: a whole 2x2x4 slice. The times are simulated.
32 devices in a mesh: seq: 8 (over z, y), mp: 4 (over x, core).
Axes of the slice: x: 2, y: 2, z: 4, core: 2. Of those that a mesh axis runs over, the one named last changes fastest.
Arguments:
- y_first: bfloat16 [2048, 896], P('seq', 'mp'), may hold values from -6 to 6
- y_second: bfloat16 [2048, 896], P('seq', 'mp'), may hold values from -10 to 10
- grad_first: bfloat16 [2048, 896], P('seq', 'mp'), may hold values from -6 to 6
- grad_second: bfloat16 [2048, 896], P('seq', 'mp'), may hold values from -6 to 6
- doc_blocks: int32 [12], replicated, may hold values from 1 to 2, as said below
- last_fill: int32 [12], replicated, may hold values from 1 to 128
- plan: int32 [16], replicated, may hold values from 0 to 15, as said below
- q_weight: bfloat16 [896, 512], P(None, 'mp'), may hold values from -1 to 1
- kv_weight: bfloat16 [2, 896, 128], P(None, 'mp'), may hold values from -1 to 1
- out_weight: bfloat16 [512, 896], P('mp'), may hold values from -0.25 to 0.25
- gate_up: bfloat16 [2, 896, 2560], P(None, None, 'mp'), may hold values from -0.1875 to 0.1875
- down_weight: bfloat16 [2560, 896], P('mp'), may hold values from -0.125 to 0.125
Outputs:
- first_input: bfloat16 [2048, 896], P('seq', 'mp')
- second_input: bfloat16 [2048, 896], P('seq', 'mp')
- first_grad: bfloat16 [2048, 896], P('seq', 'mp')
- second_grad: bfloat16 [2048, 896], P('seq', 'mp')
- q_weight_grad: float32 [896, 512], P('seq', 'mp')
- kv_weight_grad: float32 [2, 896, 128], P(None, 'seq')
- out_weight_grad: float32 [512, 896], P('mp', 'seq')
Inputs may be any that keep to these rules, and one draw needn't show every extreme that they name: `doc_blocks`: each document holds 1 or 2 blocks; together they fill all 16 blocks; exactly 4 documents hold 2. A permutation: block b goes to slot plan[b]; slots k * 2 to (k + 1) * 2 - 1 belong to index k of seq; the blocks of one document go to consecutive slots of one index, in order, the first at an even slot.
All inputs are finite; a program needn't handle non-finite values.
Results may differ from a plain program's by a relative error of at most 0.024.
Values may be sent and summed in bfloat16 or wider, within the bound.
A program may use at most 64 MiB of HBM per device.

v0:
```python
import math
import jax
import jax.numpy as jnp
from jax import lax
from jax.sharding import PartitionSpec as P

BLOCK = 128
EPSILON = 1e-06


def for_sending(value):
    return jax.tree.map(lambda a: a.astype(jnp.bfloat16) if a.dtype == jnp.float32 else a, value)


def normalize(values):
    inverse = lax.rsqrt(jnp.mean(values * values, axis=-1, keepdims=True) + EPSILON)
    return (values * inverse, inverse)


def block_table(doc_blocks, last_fill, block_count):
    doc_count = doc_blocks.shape[0]
    starts = jnp.cumsum(doc_blocks) - doc_blocks
    index = jnp.arange(block_count, dtype=jnp.int32)
    owner_doc = jnp.sum((starts[None, :] <= index[:, None]).astype(jnp.int32), axis=1) - 1
    onehot = (owner_doc[:, None] == jnp.arange(doc_count, dtype=jnp.int32)[None, :]).astype(
        jnp.int32
    )
    first_block = jnp.sum(onehot * starts[None, :], axis=1)
    length = jnp.sum(onehot * doc_blocks[None, :], axis=1)
    filled = jnp.sum(onehot * last_fill[None, :], axis=1)
    limit = jnp.where(index - first_block == length - 1, filled, BLOCK)
    return (owner_doc, limit)


def attend_mask(doc_rows, valid_rows):
    count = doc_rows.shape[-1]
    order = jnp.arange(count, dtype=jnp.int32)
    causal = order[None, :] <= order[:, None]
    same_doc = doc_rows[..., :, None] == doc_rows[..., None, :]
    keep = valid_rows[..., None, :] | (order[None, :] == order[:, None])
    return same_doc & causal & keep


def contract_last(left, right):
    return lax.dot_general(
        left, right, (((1,), (1,)), ((), ())), preferred_element_type=jnp.float32
    )


def contract_first(left, right):
    return lax.dot_general(
        left, right, (((0,), (0,)), ((), ())), preferred_element_type=jnp.float32
    )


def to_owners(streams, source):
    pieces = lax.axis_size("seq")
    row_total, feat_width = streams[0].shape
    slot_count = row_total // BLOCK
    share_rows = BLOCK // pieces
    split = tuple((item.reshape(slot_count, pieces, share_rows, feat_width) for item in streams))
    held = jax.tree.map(
        lambda part, own: part.astype(own.dtype),
        lax.all_to_all(for_sending(split), "seq", split_axis=1, concat_axis=0, tiled=True),
        split,
    )
    placed = tuple(
        (item[source].reshape(pieces, slot_count, share_rows, feat_width) for item in held)
    )
    owned = jax.tree.map(
        lambda part, own: part.astype(own.dtype),
        lax.all_to_all(for_sending(placed), "seq", split_axis=0, concat_axis=2, tiled=True),
        placed,
    )
    return tuple((item.reshape(row_total, feat_width) for item in owned))


def shards(
    y_first,
    y_second,
    grad_first,
    grad_second,
    doc_blocks,
    last_fill,
    plan,
    q_weight,
    kv_weight,
    out_weight,
    gate_up,
    down_weight,
):
    f32 = jnp.float32
    bf16 = jnp.bfloat16
    block_count = plan.shape[0]
    source = (
        jnp.zeros((block_count,), jnp.int32).at[plan].set(jnp.arange(block_count, dtype=jnp.int32))
    )
    owner_doc, limit = block_table(doc_blocks, last_fill, block_count)
    moved = to_owners((y_first, y_second, grad_first, grad_second), source)
    share_width = moved[0].shape[1]
    first, second, cot_first, cot_second, kv_full = (
        lax.all_gather(moved[0], "mp", axis=1, tiled=True),
        lax.all_gather(moved[1], "mp", axis=1, tiled=True),
        lax.all_gather(moved[2], "mp", axis=1, tiled=True),
        lax.all_gather(moved[3], "mp", axis=1, tiled=True),
        lax.all_gather(kv_weight, "mp", axis=1, tiled=True),
    )
    row_total, width = first.shape
    slot_count = row_total // BLOCK
    owned_slots = lax.axis_index("seq") * slot_count + jnp.arange(slot_count, dtype=jnp.int32)
    mine = source[owned_slots]
    row_doc = jnp.repeat(owner_doc[mine], BLOCK, total_repeat_length=row_total)
    row_limit = jnp.repeat(limit[mine], BLOCK, total_repeat_length=row_total)
    valid = jnp.arange(row_total, dtype=jnp.int32) % BLOCK < row_limit
    column_start = lax.axis_index("mp") * share_width

    def own_share(values):
        return lax.dynamic_slice_in_dim(values, column_start, share_width, 1)

    n_one, r_one = normalize(first.astype(f32))
    n_one_b = n_one.astype(bf16)
    gate_pre = jnp.dot(n_one_b, gate_up[0], preferred_element_type=f32)
    up_pre = jnp.dot(n_one_b, gate_up[1], preferred_element_type=f32)
    sigma = jax.nn.sigmoid(gate_pre)
    silu_gate = gate_pre * sigma
    hidden = (silu_gate * up_pre).astype(bf16)
    mix_part = jnp.dot(hidden, down_weight, preferred_element_type=f32)
    mixed = lax.psum(mix_part, "mp")
    second_in = (second.astype(f32) - mixed).astype(bf16)
    d_hidden = contract_last(cot_second, down_weight)
    d_gate = (d_hidden * up_pre * sigma * (1.0 + gate_pre * (1.0 - sigma))).astype(bf16)
    d_up = (d_hidden * silu_gate).astype(bf16)
    norm_part = contract_last(d_gate, gate_up[0]) + contract_last(d_up, gate_up[1])
    norm_share = lax.psum_scatter(
        norm_part.astype(jnp.bfloat16), "mp", scatter_dimension=1, tiled=True
    ).astype(jnp.float32)
    n_one_share = own_share(n_one)
    inner = lax.psum(jnp.sum(norm_share * n_one_share, axis=1, keepdims=True), "mp") / width
    first_share = (moved[2].astype(f32) + (norm_share - n_one_share * inner) * r_one).astype(bf16)
    first_cot = lax.all_gather(first_share, "mp", axis=1, tiled=True)
    kv_count = kv_full.shape[0]
    head_size = kv_full.shape[2] // 2
    local_heads = q_weight.shape[1] // head_size
    per_group = local_heads * lax.axis_size("mp") // kv_count
    group = lax.axis_index("mp") * local_heads // per_group
    kv_local = lax.dynamic_index_in_dim(kv_full, group, 0, keepdims=False)
    n_two, r_two = normalize(second_in.astype(f32))
    n_two_b = n_two.astype(bf16)
    query = jnp.dot(n_two_b, q_weight, preferred_element_type=f32).astype(bf16)
    keyval = jnp.dot(n_two_b, kv_local, preferred_element_type=f32).astype(bf16)
    pair_rows = 2 * BLOCK
    pair_count = row_total // pair_rows
    query_groups = query.reshape(pair_count, pair_rows, local_heads, head_size)
    key_groups = keyval[:, :head_size].reshape(pair_count, pair_rows, head_size)
    value_groups = keyval[:, head_size:].reshape(pair_count, pair_rows, head_size)
    allowed = attend_mask(
        row_doc.reshape(pair_count, pair_rows), valid.reshape(pair_count, pair_rows)
    )
    scale = 1.0 / math.sqrt(head_size)
    scores = (
        jnp.einsum("gihd,gjd->ghij", query_groups, key_groups, preferred_element_type=f32) * scale
    )
    scores = jnp.where(allowed[:, None], scores, -1e30)
    highest = jnp.max(scores, axis=-1, keepdims=True)
    expo = jnp.exp(scores - highest)
    probs = expo / jnp.sum(expo, axis=-1, keepdims=True)
    probs_b = probs.astype(bf16)
    heads_out = (
        jnp.einsum("ghij,gjd->gihd", probs_b, value_groups, preferred_element_type=f32)
        .astype(bf16)
        .reshape(row_total, local_heads * head_size)
    )
    attn = lax.psum(
        jnp.dot(heads_out, out_weight, preferred_element_type=f32).astype(jnp.bfloat16), "mp"
    ).astype(jnp.float32)
    live = valid[:, None]
    first_in = (first.astype(f32) - live.astype(f32) * attn).astype(bf16)
    masked_cot = first_cot * live.astype(bf16)
    out_grad = contract_first(heads_out, masked_cot)
    d_out = (
        contract_last(masked_cot, out_weight)
        .astype(bf16)
        .reshape(pair_count, pair_rows, local_heads, head_size)
    )
    d_prob = jnp.einsum("gihd,gjd->ghij", d_out, value_groups, preferred_element_type=f32)
    delta = jnp.sum(probs * d_prob, axis=-1, keepdims=True)
    d_score = (probs * (d_prob - delta) * scale).astype(bf16)
    d_query = (
        jnp.einsum("ghij,gjd->gihd", d_score, key_groups, preferred_element_type=f32)
        .astype(bf16)
        .reshape(row_total, local_heads * head_size)
    )
    d_key = jnp.einsum("ghij,gihd->gjhd", d_score, query_groups, preferred_element_type=f32).astype(
        bf16
    )
    d_value = jnp.einsum("ghij,gihd->gjhd", probs_b, d_out, preferred_element_type=f32).astype(bf16)
    q_grad = contract_first(n_two_b, d_query)
    norm_groups = n_two_b.reshape(pair_count, pair_rows, width)
    key_grad = jnp.einsum("gsk,gshd->kd", norm_groups, d_key, preferred_element_type=f32)
    value_grad = jnp.einsum("gsk,gshd->kd", norm_groups, d_value, preferred_element_type=f32)
    kv_own = jnp.concatenate([key_grad, value_grad], axis=1)
    d_norm_two = contract_last(d_query, q_weight)
    d_norm_two = d_norm_two + jnp.einsum(
        "gshd,kd->gsk", d_key, kv_local[:, :head_size], preferred_element_type=f32
    ).reshape(row_total, width)
    d_norm_two = d_norm_two + jnp.einsum(
        "gshd,kd->gsk", d_value, kv_local[:, head_size:], preferred_element_type=f32
    ).reshape(row_total, width)
    d_norm_two = lax.psum(d_norm_two.astype(jnp.bfloat16), "mp").astype(jnp.float32)
    inner_two = jnp.mean(d_norm_two * n_two, axis=-1, keepdims=True)
    second_cot = (cot_second.astype(f32) + (d_norm_two - n_two * inner_two) * r_two).astype(bf16)
    q_share = lax.psum_scatter(q_grad, "seq", scatter_dimension=0, tiled=True)
    kv_grad = jnp.zeros((kv_count, width, 2 * head_size), f32)
    kv_grad = lax.dynamic_update_index_in_dim(kv_grad, kv_own, group, 0)
    out_share, kv_part = (
        lax.psum_scatter(out_grad, "seq", scatter_dimension=1, tiled=True),
        lax.psum_scatter(kv_grad, "seq", scatter_dimension=1, tiled=True),
    )
    kv_share = lax.psum(kv_part, "mp")
    return (
        own_share(first_in),
        own_share(second_in),
        first_share,
        own_share(second_cot),
        q_share,
        kv_share,
        out_share,
    )


def solution(mesh):
    return jax.shard_map(
        shards,
        mesh=mesh,
        in_specs=(
            P("seq", "mp"),
            P("seq", "mp"),
            P("seq", "mp"),
            P("seq", "mp"),
            P(),
            P(),
            P(),
            P(None, "mp"),
            P(None, "mp", None),
            P("mp", None),
            P(None, None, "mp"),
            P("mp", None),
        ),
        out_specs=(
            P("seq", "mp"),
            P("seq", "mp"),
            P("seq", "mp"),
            P("seq", "mp"),
            P("seq", "mp"),
            P(None, "seq", None),
            P("mp", "seq"),
        ),
        check_vma=False,
    )
```

profile of v0, /device:TPU:0, one launch (start us, length us, event | category | flops | bytes accessed | tf_op | source)
XLA Modules:
  0.0 467.6 jit_solution(3869260832934583238)
XLA Ops:
  9.0 7.3 %all-to-all-start = ((bf16[2,8,16,224]{3,2,0,1:T(8,128)(2,1)}), bf16[2,8,16,224]{3,2,0,1:T(8,128)(2,1)S(1)}, u32[]{:S(2)}, u32[]{:S(2)}) async-start(bf16[2,8,16,224]{3,2,0,1:T(8,128)(2,1)} %copy.94), calls=%async_computation | async-start | bytes 262144 | tf_op jit(solution)/shard_map/all_to_all | solution.py:64
  23.6 5.5 %all-to-all-start.6 = ((bf16[2,8,16,224]{3,2,0,1:T(8,128)(2,1)}), bf16[2,8,16,224]{3,2,0,1:T(8,128)(2,1)S(1)}, u32[]{:S(2)}, u32[]{:S(2)}) async-start(bf16[2,8,16,224]{3,2,0,1:T(8,128)(2,1)} %copy.107), calls=%async_computation.6 | async-start | bytes 262144 | tf_op jit(solution)/shard_map/all_to_all | solution.py:64
  29.7 6.8 %all-to-all-done.6 = bf16[2,8,16,224]{3,2,0,1:T(8,128)(2,1)S(1)} async-done(((bf16[2,8,16,224]{3,2,0,1:T(8,128)(2,1)}), bf16[2,8,16,224]{3,2,0,1:T(8,128)(2,1)S(1)}, u32[]{:S(2)}, u32[]{:S(2)}) %all-to-all-start.6) | async-done | bytes 114720 | tf_op jit(solution)/shard_map/all_to_all | solution.py:64
  36.5 3.4 all-to-all-start.4
  42.0 6.8 %all_gather.17 = bf16[2,896,128]{2,1,0:T(8,128)(2,1)S(1)} all-gather(bf16[2,224,128]{2,1,0:T(8,128)(2,1)S(1)} %copy-done.16), channel_id=1, replica_groups=mesh['seq'=8,'mp'=4] {'mp'}, dimensions={1}, use_global_device_ids=true | all-gather | bytes 573440 | tf_op jit(solution)/shard_map/all_gather | solution.py:106
  48.8 5.9 %all-to-all-start.2 = ((bf16[2,8,16,224]{3,2,0,1:T(8,128)(2,1)}), bf16[2,8,16,224]{3,2,0,1:T(8,128)(2,1)S(1)}, u32[]{:S(2)}, u32[]{:S(2)}) async-start(bf16[2,8,16,224]{3,2,0,1:T(8,128)(2,1)} %copy.98), calls=%async_computation.2 | async-start | bytes 262144 | tf_op jit(solution)/shard_map/all_to_all | solution.py:64
  57.2 5.0 %all-to-all-done.2 = bf16[2,8,16,224]{3,2,0,1:T(8,128)(2,1)S(1)} async-done(((bf16[2,8,16,224]{3,2,0,1:T(8,128)(2,1)}), bf16[2,8,16,224]{3,2,0,1:T(8,128)(2,1)S(1)}, u32[]{:S(2)}, u32[]{:S(2)}) %all-to-all-start.2) | async-done | bytes 114720 | tf_op jit(solution)/shard_map/all_to_all | solution.py:64
  62.2 3.4 all-to-all-start.1
  69.9 2.9 all-to-all-done.1
  72.8 3.4 all-to-all-start.7
  76.4 6.3 %all_gather.15 = bf16[256,896]{0,1:T(8,128)(2,1)S(1)} all-gather(bf16[256,224]{0,1:T(8,128)(2,1)S(1)} %copy.96), channel_id=1, replica_groups=mesh['seq'=8,'mp'=4] {'mp'}, dimensions={1}, use_global_device_ids=true | all-gather | bytes 573440 | tf_op jit(solution)/shard_map/all_gather | solution.py:102
  82.8 2.8 fusion.9
  87.1 5.9 %all-to-all-start.5 = ((bf16[8,2,16,224]{3,2,1,0:T(8,128)(2,1)}), bf16[8,2,16,224]{3,2,1,0:T(8,128)(2,1)S(1)}, u32[]{:S(2)}, u32[]{:S(2)}) async-start(bf16[8,2,16,224]{3,2,1,0:T(8,128)(2,1)} %bitcast.42), calls=%async_computation.5 | async-start | bytes 262144 | tf_op jit(solution)/shard_map/all_to_all | solution.py:72
  93.2 6.8 %all_gather.18 = bf16[256,896]{0,1:T(8,128)(2,1)S(1)} all-gather(bf16[256,224]{0,1:T(8,128)(2,1)S(1)} %copy.109), channel_id=1, replica_groups=mesh['seq'=8,'mp'=4] {'mp'}, dimensions={1}, use_global_device_ids=true | all-gather | bytes 573440 | tf_op jit(solution)/shard_map/all_gather | solution.py:105
  100.6 3.2 fusion.7
  103.8 1.5 fusion.26
  105.4 5.7 %all-to-all-start.3 = ((bf16[8,2,16,224]{3,2,1,0:T(8,128)(2,1)}), bf16[8,2,16,224]{3,2,1,0:T(8,128)(2,1)S(1)}, u32[]{:S(2)}, u32[]{:S(2)}) async-start(bf16[8,2,16,224]{3,2,1,0:T(8,128)(2,1)} %bitcast.20), calls=%async_computation.3 | async-start | bytes 262144 | tf_op jit(solution)/shard_map/all_to_all | solution.py:72
  112.9 5.7 %all-to-all-done.3 = bf16[8,2,16,224]{3,2,1,0:T(8,128)(2,1)S(1)} async-done(((bf16[8,2,16,224]{3,2,1,0:T(8,128)(2,1)}), bf16[8,2,16,224]{3,2,1,0:T(8,128)(2,1)S(1)}, u32[]{:S(2)}, u32[]{:S(2)}) %all-to-all-start.3) | async-done | bytes 114720 | tf_op jit(solution)/shard_map/all_to_all | solution.py:72
  118.7 8.9 %all_gather.16 = bf16[256,896]{0,1:T(8,128)(2,1)S(1)} all-gather(bf16[256,224]{0,1:T(8,128)(2,1)S(1)} %copy.100), channel_id=1, replica_groups=mesh['seq'=8,'mp'=4] {'mp'}, dimensions={1}, use_global_device_ids=true | all-gather | bytes 573440 | tf_op jit(solution)/shard_map/all_gather | solution.py:103
  127.8 3.4 fusion.1
  131.3 19.7 %all-reduce.5.cloned.1.call-done = f32[256,896]{1,0:T(8,128)} async-done(((f32[256,896]{1,0:T(8,128)}), f32[256,896]{1,0:T(8,128)}) %all-reduce.5.cloned.1.call-update) | async-done | bytes 917520 | tf_op jit(solution)/shard_map/psum | solution.py:128
  156.9 17.9 %reduce-scatter.5.cloned.1.call-done = bf16[256,224]{0,1:T(8,128)(2,1)} async-done(((bf16[256,896]{0,1:T(8,128)(2,1)}), bf16[256,224]{0,1:T(8,128)(2,1)}) %reduce-scatter.5.cloned.1.call-update) | async-done | bytes 114704 | tf_op jit(solution)/shard_map/reduce_scatter | solution.py:134
  175.9 5.8 %psum.37 = f32[256,1]{0,1:T(1,128)S(1)} all-reduce(f32[256,1]{0,1:T(1,128)S(1)} %bitcast.175), channel_id=1, replica_groups=mesh['seq'=8,'mp'=4] {'mp'}, use_global_device_ids=true, to_apply=%region_14.16 | all-reduce | flops 256 | bytes 2048 | tf_op jit(solution)/shard_map/psum | solution.py:138
  182.8 6.5 %all_gather.19 = bf16[256,896]{0,1:T(8,128)(2,1)S(1)} all-gather(bf16[256,224]{0,1:T(8,128)(2,1)S(1)} %fusion.40), channel_id=1, replica_groups=mesh['seq'=8,'mp'=4] {'mp'}, dimensions={1}, use_global_device_ids=true | all-gather | bytes 573440 | tf_op jit(solution)/shard_map/all_gather | solution.py:140
  196.9 2.1 fusion.23
  202.1 27.5 %all-reduce.9.cloned.1.call-done = (bf16[256,896]{0,1:T(8,128)(2,1)}, bf16[256,896]{1,0:T(8,128)(2,1)}) async-done(((bf16[256,896]{0,1:T(8,128)(2,1)}, bf16[256,896]{1,0:T(8,128)(2,1)}), (bf16[256,896]{0,1:T(8,128)(2,1)}, bf16[256,896]{1,0:T(8,128)(2,1)})) %all-reduce.9.cloned.1.call-update) | async-done | bytes 917520 | tf_op jit(solution)/shard_map/psum | solution.py:173
  231.4 65.5 %reduce-scatter.9.cloned.1.call-done = f32[2,112,128]{2,1,0:T(8,128)} async-done(((f32[2,896,128]{2,1,0:T(8,128)}), f32[2,112,128]{2,1,0:T(8,128)}) %reduce-scatter.9.cloned.1.call-update) | async-done | bytes 114704 | tf_op jit(solution)/shard_map/reduce_scatter | solution.py:217
  296.9 1.6 fusion.43
  299.3 62.8 %reduce-scatter.11.cloned.1.call-done = f32[128,112]{0,1:T(8,128)} async-done(((f32[128,896]{0,1:T(8,128)}), f32[128,112]{0,1:T(8,128)}) %reduce-scatter.11.cloned.1.call-update) | async-done | bytes 57360 | tf_op jit(solution)/shard_map/reduce_scatter | solution.py:216
  362.1 65.3 %reduce-scatter.7.cloned.1.call-done = f32[112,128]{1,0:T(8,128)} async-done(((f32[896,128]{1,0:T(8,128)}), f32[112,128]{1,0:T(8,128)}) %reduce-scatter.7.cloned.1.call-update) | async-done | bytes 57360 | tf_op jit(solution)/shard_map/reduce_scatter | solution.py:212
  427.4 31.8 %all-reduce.7.cloned.1.call-done = f32[2,112,128]{2,1,0:T(8,128)} async-done(((f32[2,112,128]{2,1,0:T(8,128)}), f32[2,112,128]{2,1,0:T(8,128)}) %all-reduce.7.cloned.1.call-update) | async-done | bytes 114704 | tf_op jit(solution)/shard_map/psum | solution.py:219
  459.2 1.6 copy.128
  (167 shorter events, 44.2 us)
Async XLA Ops:
  7.2 92.8 %copy-start = (bf16[640,896]{1,0:T(8,128)(2,1)S(1)}, bf16[640,896]{1,0:T(8,128)(2,1)}, u32[]{:S(2)}) copy-start(bf16[640,896]{1,0:T(8,128)(2,1)} %param.29) | copy-start | bytes 3440644
  7.2 11.4 %copy-start.14 = (bf16[256,224]{0,1:T(8,128)(2,1)S(1)}, bf16[256,224]{0,1:T(8,128)(2,1)}, u32[]{:S(2)}) copy-start(bf16[256,224]{0,1:T(8,128)(2,1)} %param.20) | copy-start | bytes 344068
  7.2 12.2 %copy-start.24 = (s32[12]{0:T(128)S(1)}, s32[12]{0:T(128)}, u32[]{:S(2)}) copy-start(s32[12]{0:T(128)} %param.22) | copy-start | bytes 148
  7.2 13.8 %copy-start.25 = (s32[12]{0:T(128)S(1)}, s32[12]{0:T(128)}, u32[]{:S(2)}) copy-start(s32[12]{0:T(128)} %param.23) | copy-start | bytes 148
  9.0 14.7 %all-to-all-start = ((bf16[2,8,16,224]{3,2,0,1:T(8,128)(2,1)}), bf16[2,8,16,224]{3,2,0,1:T(8,128)(2,1)S(1)}, u32[]{:S(2)}, u32[]{:S(2)}) async-start(bf16[2,8,16,224]{3,2,0,1:T(8,128)(2,1)} %copy.94), calls=%async_computation | async-start | bytes 262144 | tf_op jit(solution)/shard_map/all_to_all | solution.py:64
  19.4 21.8 %copy-start.15 = (bf16[256,224]{0,1:T(8,128)(2,1)S(1)}, bf16[256,224]{0,1:T(8,128)(2,1)}, u32[]{:S(2)}) copy-start(bf16[256,224]{0,1:T(8,128)(2,1)} %param.19) | copy-start | bytes 344068
  21.0 21.0 %copy-start.16 = (bf16[2,224,128]{2,1,0:T(8,128)(2,1)S(1)}, bf16[2,224,128]{2,1,0:T(8,128)(2,1)}, u32[]{:S(2)}) copy-start(bf16[2,224,128]{2,1,0:T(8,128)(2,1)} %param.26) | copy-start | bytes 344068
  23.6 12.8 %all-to-all-start.6 = ((bf16[2,8,16,224]{3,2,0,1:T(8,128)(2,1)}), bf16[2,8,16,224]{3,2,0,1:T(8,128)(2,1)S(1)}, u32[]{:S(2)}, u32[]{:S(2)}) async-start(bf16[2,8,16,224]{3,2,0,1:T(8,128)(2,1)} %copy.107), calls=%async_computation.6 | async-start | bytes 262144 | tf_op jit(solution)/shard_map/all_to_all | solution.py:64
  36.5 12.3 %all-to-all-start.4 = ((bf16[2,8,16,224]{3,2,0,1:T(8,128)(2,1)}), bf16[2,8,16,224]{3,2,0,1:T(8,128)(2,1)S(1)}, u32[]{:S(2)}, u32[]{:S(2)}) async-start(bf16[2,8,16,224]{3,2,0,1:T(8,128)(2,1)} %copy.104), calls=%async_computation.4 | async-start | bytes 262144 | tf_op jit(solution)/shard_map/all_to_all | solution.py:64
  41.1 24.4 %copy-start.22 = (pred[256]{0:T(512)(128)(4,1)}, pred[256]{0:T(512)(128)(4,1)S(1)}, u32[]{:S(2)}) copy-start(pred[256]{0:T(512)(128)(4,1)S(1)} %get-tuple-element.69) | copy-start | bytes 772
  48.8 13.4 %all-to-all-start.2 = ((bf16[2,8,16,224]{3,2,0,1:T(8,128)(2,1)}), bf16[2,8,16,224]{3,2,0,1:T(8,128)(2,1)S(1)}, u32[]{:S(2)}, u32[]{:S(2)}) async-start(bf16[2,8,16,224]{3,2,0,1:T(8,128)(2,1)} %copy.98), calls=%async_computation.2 | async-start | bytes 262144 | tf_op jit(solution)/shard_map/all_to_all | solution.py:64
  62.2 10.7 %all-to-all-start.1 = ((bf16[8,2,16,224]{3,2,1,0:T(8,128)(2,1)}), bf16[8,2,16,224]{3,2,1,0:T(8,128)(2,1)S(1)}, u32[]{:S(2)}, u32[]{:S(2)}) async-start(bf16[8,2,16,224]{3,2,1,0:T(8,128)(2,1)} %bitcast.4), calls=%async_computation.1 | async-start | bytes 262144 | tf_op jit(solution)/shard_map/all_to_all | solution.py:72
  72.8 14.3 %all-to-all-start.7 = ((bf16[8,2,16,224]{3,2,1,0:T(8,128)(2,1)}), bf16[8,2,16,224]{3,2,1,0:T(8,128)(2,1)S(1)}, u32[]{:S(2)}, u32[]{:S(2)}) async-start(bf16[8,2,16,224]{3,2,1,0:T(8,128)(2,1)} %bitcast.50), calls=%async_computation.7 | async-start | bytes 262144 | tf_op jit(solution)/shard_map/all_to_all | solution.py:72
  82.8 2.8 copy-start.26
  87.1 18.2 %all-to-all-start.5 = ((bf16[8,2,16,224]{3,2,1,0:T(8,128)(2,1)}), bf16[8,2,16,224]{3,2,1,0:T(8,128)(2,1)S(1)}, u32[]{:S(2)}, u32[]{:S(2)}) async-start(bf16[8,2,16,224]{3,2,1,0:T(8,128)(2,1)} %bitcast.42), calls=%async_computation.5 | async-start | bytes 262144 | tf_op jit(solution)/shard_map/all_to_all | solution.py:72
  93.2 7.4 %copy-start.27 = (bf16[2,896,640]{2,1,0:T(8,128)(2,1)S(1)}, bf16[2,896,640]{2,1,0:T(8,128)(2,1)}, u32[]{:S(2)}) copy-start(bf16[2,896,640]{2,1,0:T(8,128)(2,1)} %param.28) | copy-start | bytes 6881284
  100.6 4.8 %copy-start.5 = (f32[256,640]{1,0:T(8,128)}, f32[256,640]{1,0:T(8,128)S(1)}, u32[]{:S(2)}) copy-start(f32[256,640]{1,0:T(8,128)S(1)} %fusion.76) | copy-start | bytes 1966084
  100.6 3.2 copy-start.28
  100.6 3.2 copy-start.29
  105.4 13.2 %all-to-all-start.3 = ((bf16[8,2,16,224]{3,2,1,0:T(8,128)(2,1)}), bf16[8,2,16,224]{3,2,1,0:T(8,128)(2,1)S(1)}, u32[]{:S(2)}, u32[]{:S(2)}) async-start(bf16[8,2,16,224]{3,2,1,0:T(8,128)(2,1)} %bitcast.20), calls=%async_computation.3 | async-start | bytes 262144 | tf_op jit(solution)/shard_map/all_to_all | solution.py:72
  111.1 39.9 %all-reduce.5.cloned.1.call-start = ((), (), s32[]{:S(2)}) async-start(), calls=%async_computation.12 | async-start | bytes 1835008 | tf_op jit(solution)/shard_map/psum | solution.py:128
  111.8 63.0 %reduce-scatter.5.cloned.1.call-start = ((), (), s32[]{:S(2)}) async-start(), calls=%async_computation.13 | async-start | bytes 573440 | tf_op jit(solution)/shard_map/reduce_scatter | solution.py:134
  131.2 98.4 %all-reduce.9.cloned.1.call-start = ((), (), s32[]{:S(2)}) async-start(), calls=%async_computation.18 | async-start | bytes 1835008 | tf_op jit(solution)/shard_map/psum | solution.py:173
  152.8 2.3 copy-start.20
  181.7 7.6 %copy-start.13 = (bf16[128,896]{1,0:T(8,128)(2,1)S(1)}, bf16[128,896]{1,0:T(8,128)(2,1)}, u32[]{:S(2)}) copy-start(bf16[128,896]{1,0:T(8,128)(2,1)} %param.27) | copy-start | bytes 688132
  181.7 7.9 %copy-start.21 = (bf16[256,128]{0,1:T(8,128)(2,1)S(1)}, bf16[256,128]{0,1:T(8,128)(2,1)}, u32[]{:S(2)}) copy-start(bf16[256,128]{0,1:T(8,128)(2,1)} %copy-done.20) | copy-start | bytes 196612
  182.8 7.0 %copy-start.8 = (bf16[256,224]{0,1:T(8,128)(2,1)}, bf16[256,224]{0,1:T(8,128)(2,1)S(1)}, u32[]{:S(2)}) copy-start(bf16[256,224]{0,1:T(8,128)(2,1)S(1)} %fusion.40) | copy-start | bytes 344068
  193.4 103.5 %reduce-scatter.9.cloned.1.call-start = ((), (), s32[]{:S(2)}) async-start(), calls=%async_computation.15 | async-start | bytes 1032192 | tf_op jit(solution)/shard_map/reduce_scatter | solution.py:217
  195.9 3.2 copy-start.23
  196.8 165.3 %reduce-scatter.11.cloned.1.call-start = ((), (), s32[]{:S(2)}) async-start(), calls=%async_computation.17 | async-start | bytes 516096 | tf_op jit(solution)/shard_map/reduce_scatter | solution.py:216
  199.0 228.4 %reduce-scatter.7.cloned.1.call-start = ((), (), s32[]{:S(2)}) async-start(), calls=%async_computation.14 | async-start | bytes 516096 | tf_op jit(solution)/shard_map/reduce_scatter | solution.py:212
  201.0 258.1 %all-reduce.7.cloned.1.call-start = ((), (), s32[]{:S(2)}) async-start(), calls=%async_computation.16 | async-start | bytes 229376 | tf_op jit(solution)/shard_map/psum | solution.py:219
  (13 other events, 13.1 us)
Sparse Core Ops, SparseCore 0:
  114.3 36.6 all-reduce.4
  153.5 21.3 reduce-scatter.4
  193.5 36.0 all-reduce.8
  232.8 64.0 reduce-scatter.8
  300.6 61.4 reduce-scatter.10
  365.8 61.5 reduce-scatter.6
  429.7 29.4 all-reduce.6
where the time goes:
time: 469 us; the launch traced here: 468 us
  waiting for transfers between devices  312 us (67%)
  blocking collectives  41 us (9%)
  starting transfers between devices  40.8 us (9%)
  matrix products  23.1 us (5%)
  local copies, waits for them, and re-layouts  22.9 us (5%)
  between operations  14.8 us (3%)
  other arithmetic  13 us (3%)
    reduce_scatter x1, waiting for transfers between devices, shards(): lax.psum_scatter(kv_grad, 'seq', scatter_dimension=1, tiled=True)  65.5 us
    reduce_scatter x1, waiting for transfers between devices, shards(): q_share = lax.psum_scatter(q_grad, 'seq', scatter_dimension=0, tiled=True)  65.3 us
    reduce_scatter x1, waiting for transfers between devices, shards(): lax.psum_scatter(out_grad, 'seq', scatter_dimension=1, tiled=True)  62.8 us
    psum x1, waiting for transfers between devices, shards(): kv_share = lax.psum(kv_part, 'mp')  31.8 us
    psum x1, waiting for transfers between devices, shards(): lax.psum(jnp.dot(heads_out, out_weight, preferred_element_type=f32).astyp...  27.5 us
    all_to_all x4, starting transfers between devices, to_owners(): lax.all_to_all(for_sending(split), 'seq', split_axis=1, concat_axis=0, ti...  22.1 us
    psum x1, waiting for transfers between devices, shards(): mixed = lax.psum(mix_part, 'mp')  19.7 us
    all_to_all x4, starting transfers between devices, to_owners(): lax.all_to_all(for_sending(placed), 'seq', split_axis=0, concat_axis=2, t...  18.4 us
  transfers between devices with their start and end apart: 15, of which 12 were waited for; matrix products, arithmetic and copies ran while one was open for 10% of the time, Pallas kernels for 0%

commit v1 on v0

--- a/solution.py
+++ b/solution.py
@@ -216,7 +216,8 @@
         lax.psum_scatter(out_grad, "seq", scatter_dimension=1, tiled=True),
         lax.psum_scatter(kv_grad, "seq", scatter_dimension=1, tiled=True),
     )
-    kv_share = lax.psum(kv_part, "mp")
+    parts = lax.all_gather(kv_part, "mp")
+    kv_share = jnp.sum(parts, axis=0)
     return (
         own_share(first_in),
         own_share(second_in),

time: 469 us -> 449 us (0.957)
  waiting for transfers between devices: 312 us -> 274 us
  local copies, waits for them, and re-layouts: 22.9 us -> 32.3 us
  blocking collectives: 41 us -> 47.8 us
    unnamed x7, waiting for transfers between devices: 0.6 us -> 76.9 us
    reduce_scatter x1 -> x0, waiting for transfers between devices: 65.5 us -> none  [shards(): lax.psum_scatter(kv_grad, 'seq', scatter_dimension=1, tiled=True)]
    psum x1 -> x0, waiting for transfers between devices: 31.8 us -> none  [shards(): kv_share = lax.psum(kv_part, 'mp')]
    psum x1, waiting for transfers between devices: 27.5 us -> 16.4 us  [shards(): lax.psum(jnp.dot(heads_out, out_weight, preferred_element_type=f32).astyp...]
    dynamic_update_slice x1, local copies, waits for them, and re-layouts: 0.03 us -> 10.8 us  [shards(): kv_grad = lax.dynamic_update_index_in_dim(kv_grad, kv_own, group, 0)]
    all_gather x0 -> x1, blocking collectives: none -> 6.79 us  [shards(): parts = lax.all_gather(kv_part, 'mp')]
    reduce_scatter x1, waiting for transfers between devices: 62.8 us -> 56.7 us  [shards(): lax.psum_scatter(out_grad, 'seq', scatter_dimension=1, tiled=True)]
    unnamed x68 -> x59, local copies, waits for them, and re-layouts: 9.81 us -> 8.12 us
  transfers between devices with their start and end apart: 15 -> 14, of which waited for: 12 -> 11; matrix products, arithmetic and copies ran while one was open for 10% -> 13% of each run, Pallas kernels for 0% -> 0%
where the time goes in v1:
time: 449 us; the launch traced here: 447 us
  waiting for transfers between devices  274 us (61%)
  blocking collectives  47.8 us (11%)
  starting transfers between devices  40.9 us (9%)
  local copies, waits for them, and re-layouts  32.3 us (7%)
  matrix products  23.1 us (5%)
  between operations  15.4 us (3%)
  other arithmetic  13.6 us (3%)
    unnamed x7, waiting for transfers between devices  76.9 us
    reduce_scatter x1, waiting for transfers between devices, shards(): q_share = lax.psum_scatter(q_grad, 'seq', scatter_dimension=0, tiled=True)  65.3 us
    reduce_scatter x1, waiting for transfers between devices, shards(): lax.psum_scatter(out_grad, 'seq', scatter_dimension=1, tiled=True)  56.7 us
    all_to_all x4, starting transfers between devices, to_owners(): lax.all_to_all(for_sending(split), 'seq', split_axis=1, concat_axis=0, ti...  22.1 us
    psum x1, waiting for transfers between devices, shards(): mixed = lax.psum(mix_part, 'mp')  19.7 us
    all_to_all x4, starting transfers between devices, to_owners(): lax.all_to_all(for_sending(placed), 'seq', split_axis=0, concat_axis=2, t...  18.4 us
    reduce_scatter x1, waiting for transfers between devices, shards(): lax.psum_scatter(norm_part.astype(jnp.bfloat16), 'mp', scatter_dimension=...  17.9 us
    psum x1, waiting for transfers between devices, shards(): lax.psum(jnp.dot(heads_out, out_weight, preferred_element_type=f32).astyp...  16.4 us
  transfers between devices with their start and end apart: 14, of which 11 were waited for; matrix products, arithmetic and copies ran while one was open for 13% of the time, Pallas kernels for 0%

profile of v1, /device:TPU:0, one launch (start us, length us, event | category | flops | bytes accessed | tf_op | source)
XLA Modules:
  0.0 446.9 jit_solution(10006467370226616929)
XLA Ops:
  9.0 7.3 %all-to-all-start = ((bf16[2,8,16,224]{3,2,0,1:T(8,128)(2,1)}), bf16[2,8,16,224]{3,2,0,1:T(8,128)(2,1)S(1)}, u32[]{:S(2)}, u32[]{:S(2)}) async-start(bf16[2,8,16,224]{3,2,0,1:T(8,128)(2,1)} %copy.98), calls=%async_computation | async-start | bytes 262144 | tf_op jit(solution)/shard_map/all_to_all | solution.py:64
  23.6 5.5 %all-to-all-start.6 = ((bf16[2,8,16,224]{3,2,0,1:T(8,128)(2,1)}), bf16[2,8,16,224]{3,2,0,1:T(8,128)(2,1)S(1)}, u32[]{:S(2)}, u32[]{:S(2)}) async-start(bf16[2,8,16,224]{3,2,0,1:T(8,128)(2,1)} %copy.111), calls=%async_computation.6 | async-start | bytes 262144 | tf_op jit(solution)/shard_map/all_to_all | solution.py:64
  29.7 6.8 %all-to-all-done.6 = bf16[2,8,16,224]{3,2,0,1:T(8,128)(2,1)S(1)} async-done(((bf16[2,8,16,224]{3,2,0,1:T(8,128)(2,1)}), bf16[2,8,16,224]{3,2,0,1:T(8,128)(2,1)S(1)}, u32[]{:S(2)}, u32[]{:S(2)}) %all-to-all-start.6) | async-done | bytes 114720 | tf_op jit(solution)/shard_map/all_to_all | solution.py:64
  36.5 3.4 all-to-all-start.4
  41.9 6.8 %all_gather.23 = bf16[2,896,128]{2,1,0:T(8,128)(2,1)S(1)} all-gather(bf16[2,224,128]{2,1,0:T(8,128)(2,1)S(1)} %copy-done.12), channel_id=1, replica_groups=mesh['seq'=8,'mp'=4] {'mp'}, dimensions={1}, use_global_device_ids=true | all-gather | bytes 573440 | tf_op jit(solution)/shard_map/all_gather | solution.py:106
  48.7 5.9 %all-to-all-start.2 = ((bf16[2,8,16,224]{3,2,0,1:T(8,128)(2,1)}), bf16[2,8,16,224]{3,2,0,1:T(8,128)(2,1)S(1)}, u32[]{:S(2)}, u32[]{:S(2)}) async-start(bf16[2,8,16,224]{3,2,0,1:T(8,128)(2,1)} %copy.102), calls=%async_computation.2 | async-start | bytes 262144 | tf_op jit(solution)/shard_map/all_to_all | solution.py:64
  57.2 5.0 %all-to-all-done.2 = bf16[2,8,16,224]{3,2,0,1:T(8,128)(2,1)S(1)} async-done(((bf16[2,8,16,224]{3,2,0,1:T(8,128)(2,1)}), bf16[2,8,16,224]{3,2,0,1:T(8,128)(2,1)S(1)}, u32[]{:S(2)}, u32[]{:S(2)}) %all-to-all-start.2) | async-done | bytes 114720 | tf_op jit(solution)/shard_map/all_to_all | solution.py:64
  62.2 3.4 all-to-all-start.1
  69.9 2.9 all-to-all-done.1
  72.8 3.4 all-to-all-start.7
  76.3 6.3 %all_gather.21 = bf16[256,896]{0,1:T(8,128)(2,1)S(1)} all-gather(bf16[256,224]{0,1:T(8,128)(2,1)S(1)} %copy.100), channel_id=1, replica_groups=mesh['seq'=8,'mp'=4] {'mp'}, dimensions={1}, use_global_device_ids=true | all-gather | bytes 573440 | tf_op jit(solution)/shard_map/all_gather | solution.py:102
  82.8 2.8 fusion.9
  87.1 5.9 %all-to-all-start.5 = ((bf16[8,2,16,224]{3,2,1,0:T(8,128)(2,1)}), bf16[8,2,16,224]{3,2,1,0:T(8,128)(2,1)S(1)}, u32[]{:S(2)}, u32[]{:S(2)}) async-start(bf16[8,2,16,224]{3,2,1,0:T(8,128)(2,1)} %bitcast.42), calls=%async_computation.5 | async-start | bytes 262144 | tf_op jit(solution)/shard_map/all_to_all | solution.py:72
  93.1 6.8 %all_gather.24 = bf16[256,896]{0,1:T(8,128)(2,1)S(1)} all-gather(bf16[256,224]{0,1:T(8,128)(2,1)S(1)} %copy.113), channel_id=1, replica_groups=mesh['seq'=8,'mp'=4] {'mp'}, dimensions={1}, use_global_device_ids=true | all-gather | bytes 573440 | tf_op jit(solution)/shard_map/all_gather | solution.py:105
  100.6 3.2 fusion.7
  103.8 1.5 fusion.26
  105.3 5.7 %all-to-all-start.3 = ((bf16[8,2,16,224]{3,2,1,0:T(8,128)(2,1)}), bf16[8,2,16,224]{3,2,1,0:T(8,128)(2,1)S(1)}, u32[]{:S(2)}, u32[]{:S(2)}) async-start(bf16[8,2,16,224]{3,2,1,0:T(8,128)(2,1)} %bitcast.20), calls=%async_computation.3 | async-start | bytes 262144 | tf_op jit(solution)/shard_map/all_to_all | solution.py:72
  112.8 5.7 %all-to-all-done.3 = bf16[8,2,16,224]{3,2,1,0:T(8,128)(2,1)S(1)} async-done(((bf16[8,2,16,224]{3,2,1,0:T(8,128)(2,1)}), bf16[8,2,16,224]{3,2,1,0:T(8,128)(2,1)S(1)}, u32[]{:S(2)}, u32[]{:S(2)}) %all-to-all-start.3) | async-done | bytes 114720 | tf_op jit(solution)/shard_map/all_to_all | solution.py:72
  118.6 8.9 %all_gather.22 = bf16[256,896]{0,1:T(8,128)(2,1)S(1)} all-gather(bf16[256,224]{0,1:T(8,128)(2,1)S(1)} %copy.104), channel_id=1, replica_groups=mesh['seq'=8,'mp'=4] {'mp'}, dimensions={1}, use_global_device_ids=true | all-gather | bytes 573440 | tf_op jit(solution)/shard_map/all_gather | solution.py:103
  127.7 3.4 fusion.1
  131.2 19.7 %all-reduce.6.cloned.1.call-done = f32[256,896]{1,0:T(8,128)} async-done(((f32[256,896]{1,0:T(8,128)}), f32[256,896]{1,0:T(8,128)}) %all-reduce.6.cloned.1.call-update) | async-done | bytes 917520 | tf_op jit(solution)/shard_map/psum | solution.py:128
  156.8 17.9 %reduce-scatter.4.cloned.1.call-done = bf16[256,224]{0,1:T(8,128)(2,1)} async-done(((bf16[256,896]{0,1:T(8,128)(2,1)}), bf16[256,224]{0,1:T(8,128)(2,1)}) %reduce-scatter.4.cloned.1.call-update) | async-done | bytes 114704 | tf_op jit(solution)/shard_map/reduce_scatter | solution.py:134
  175.8 5.8 %psum.30 = f32[256,1]{0,1:T(1,128)S(1)} all-reduce(f32[256,1]{0,1:T(1,128)S(1)} %bitcast.178), channel_id=1, replica_groups=mesh['seq'=8,'mp'=4] {'mp'}, use_global_device_ids=true, to_apply=%region_14.16 | all-reduce | flops 256 | bytes 2048 | tf_op jit(solution)/shard_map/psum | solution.py:138
  182.7 6.5 %all_gather.25 = bf16[256,896]{0,1:T(8,128)(2,1)S(1)} all-gather(bf16[256,224]{0,1:T(8,128)(2,1)S(1)} %fusion.40), channel_id=1, replica_groups=mesh['seq'=8,'mp'=4] {'mp'}, dimensions={1}, use_global_device_ids=true | all-gather | bytes 573440 | tf_op jit(solution)/shard_map/all_gather | solution.py:140
  195.2 10.8 %dynamic_update_slice.4 = f32[2,896,128]{2,0,1:T(2,128)S(1)} dynamic-update-slice(f32[2,896,128]{2,0,1:T(2,128)S(1)} %broadcast_in_dim.35, f32[1,896,128]{2,0,1:T(1,128)} %copy.119, s32[]{:T(128)S(6)} %select_n.78, s32[]{:T(128)} %constant.148.clone.1, s32[]{:T(128)} %constant.148.clone.1) | dynamic-update-slice | bytes 917508 | tf_op jit(solution)/shard_map/jit(dynamic_update_index_in_dim)/dynamic_update_slice | solution.py:214
  207.0 2.1 fusion.23
  212.8 16.4 %all-reduce.10.cloned.1.call-done = (bf16[256,896]{0,1:T(8,128)(2,1)}, bf16[256,896]{1,0:T(8,128)(2,1)}) async-done(((bf16[256,896]{0,1:T(8,128)(2,1)}, bf16[256,896]{1,0:T(8,128)(2,1)}), (bf16[256,896]{0,1:T(8,128)(2,1)}, bf16[256,896]{1,0:T(8,128)(2,1)})) %all-reduce.10.cloned.1.call-update) | async-done | bytes 917520 | tf_op jit(solution)/shard_map/psum | solution.py:173
  231.7 1.6 fusion.43
  233.3 76.4 %all-reduce.8.cloned.1.call-done = f32[2,896,128]{2,0,1:T(2,128)} async-done(((f32[2,896,128]{2,0,1:T(2,128)}), f32[2,896,128]{2,0,1:T(2,128)}) %all-reduce.8.cloned.1.call-update) | async-done | bytes 917520
  310.6 6.8 %all-gather = f32[8,112,128]{2,1,0:T(8,128)S(1)} all-gather(f32[2,112,128]{2,1,0:T(8,128)S(1)} %copy.120), channel_id=2, replica_groups=mesh['seq'=8,'mp'=4] {'mp'}, dimensions={0}, use_global_device_ids=true | all-gather | bytes 573440 | tf_op jit(solution)/shard_map/all_gather | solution.py:219
  318.1 56.7 %reduce-scatter.8.cloned.1.call-done = f32[128,112]{0,1:T(8,128)} async-done(((f32[128,896]{0,1:T(8,128)}), f32[128,112]{0,1:T(8,128)}) %reduce-scatter.8.cloned.1.call-update) | async-done | bytes 57360 | tf_op jit(solution)/shard_map/reduce_scatter | solution.py:216
  374.8 65.3 %reduce-scatter.6.cloned.1.call-done = f32[112,128]{1,0:T(8,128)} async-done(((f32[896,128]{1,0:T(8,128)}), f32[112,128]{1,0:T(8,128)}) %reduce-scatter.6.cloned.1.call-update) | async-done | bytes 57360 | tf_op jit(solution)/shard_map/reduce_scatter | solution.py:212
  (158 shorter events, 45.1 us)
Async XLA Ops:
  7.2 92.7 %copy-start = (bf16[640,896]{1,0:T(8,128)(2,1)S(1)}, bf16[640,896]{1,0:T(8,128)(2,1)}, u32[]{:S(2)}) copy-start(bf16[640,896]{1,0:T(8,128)(2,1)} %param.29) | copy-start | bytes 3440644
  7.2 11.4 %copy-start.10 = (bf16[256,224]{0,1:T(8,128)(2,1)S(1)}, bf16[256,224]{0,1:T(8,128)(2,1)}, u32[]{:S(2)}) copy-start(bf16[256,224]{0,1:T(8,128)(2,1)} %param.20) | copy-start | bytes 344068
  7.2 12.2 %copy-start.18 = (s32[12]{0:T(128)S(1)}, s32[12]{0:T(128)}, u32[]{:S(2)}) copy-start(s32[12]{0:T(128)} %param.22) | copy-start | bytes 148
  7.2 13.8 %copy-start.19 = (s32[12]{0:T(128)S(1)}, s32[12]{0:T(128)}, u32[]{:S(2)}) copy-start(s32[12]{0:T(128)} %param.23) | copy-start | bytes 148
  9.0 14.7 %all-to-all-start = ((bf16[2,8,16,224]{3,2,0,1:T(8,128)(2,1)}), bf16[2,8,16,224]{3,2,0,1:T(8,128)(2,1)S(1)}, u32[]{:S(2)}, u32[]{:S(2)}) async-start(bf16[2,8,16,224]{3,2,0,1:T(8,128)(2,1)} %copy.98), calls=%async_computation | async-start | bytes 262144 | tf_op jit(solution)/shard_map/all_to_all | solution.py:64
  19.4 21.8 %copy-start.11 = (bf16[256,224]{0,1:T(8,128)(2,1)S(1)}, bf16[256,224]{0,1:T(8,128)(2,1)}, u32[]{:S(2)}) copy-start(bf16[256,224]{0,1:T(8,128)(2,1)} %param.19) | copy-start | bytes 344068
  21.0 21.0 %copy-start.12 = (bf16[2,224,128]{2,1,0:T(8,128)(2,1)S(1)}, bf16[2,224,128]{2,1,0:T(8,128)(2,1)}, u32[]{:S(2)}) copy-start(bf16[2,224,128]{2,1,0:T(8,128)(2,1)} %param.26) | copy-start | bytes 344068
  23.6 12.8 %all-to-all-start.6 = ((bf16[2,8,16,224]{3,2,0,1:T(8,128)(2,1)}), bf16[2,8,16,224]{3,2,0,1:T(8,128)(2,1)S(1)}, u32[]{:S(2)}, u32[]{:S(2)}) async-start(bf16[2,8,16,224]{3,2,0,1:T(8,128)(2,1)} %copy.111), calls=%async_computation.6 | async-start | bytes 262144 | tf_op jit(solution)/shard_map/all_to_all | solution.py:64
  36.5 12.3 %all-to-all-start.4 = ((bf16[2,8,16,224]{3,2,0,1:T(8,128)(2,1)}), bf16[2,8,16,224]{3,2,0,1:T(8,128)(2,1)S(1)}, u32[]{:S(2)}, u32[]{:S(2)}) async-start(bf16[2,8,16,224]{3,2,0,1:T(8,128)(2,1)} %copy.108), calls=%async_computation.4 | async-start | bytes 262144 | tf_op jit(solution)/shard_map/all_to_all | solution.py:64
  48.7 13.4 %all-to-all-start.2 = ((bf16[2,8,16,224]{3,2,0,1:T(8,128)(2,1)}), bf16[2,8,16,224]{3,2,0,1:T(8,128)(2,1)S(1)}, u32[]{:S(2)}, u32[]{:S(2)}) async-start(bf16[2,8,16,224]{3,2,0,1:T(8,128)(2,1)} %copy.102), calls=%async_computation.2 | async-start | bytes 262144 | tf_op jit(solution)/shard_map/all_to_all | solution.py:64
  62.2 10.7 %all-to-all-start.1 = ((bf16[8,2,16,224]{3,2,1,0:T(8,128)(2,1)}), bf16[8,2,16,224]{3,2,1,0:T(8,128)(2,1)S(1)}, u32[]{:S(2)}, u32[]{:S(2)}) async-start(bf16[8,2,16,224]{3,2,1,0:T(8,128)(2,1)} %bitcast.4), calls=%async_computation.1 | async-start | bytes 262144 | tf_op jit(solution)/shard_map/all_to_all | solution.py:72
  72.8 14.3 %all-to-all-start.7 = ((bf16[8,2,16,224]{3,2,1,0:T(8,128)(2,1)}), bf16[8,2,16,224]{3,2,1,0:T(8,128)(2,1)S(1)}, u32[]{:S(2)}, u32[]{:S(2)}) async-start(bf16[8,2,16,224]{3,2,1,0:T(8,128)(2,1)} %bitcast.50), calls=%async_computation.7 | async-start | bytes 262144 | tf_op jit(solution)/shard_map/all_to_all | solution.py:72
  82.8 2.8 copy-start.20
  87.1 18.2 %all-to-all-start.5 = ((bf16[8,2,16,224]{3,2,1,0:T(8,128)(2,1)}), bf16[8,2,16,224]{3,2,1,0:T(8,128)(2,1)S(1)}, u32[]{:S(2)}, u32[]{:S(2)}) async-start(bf16[8,2,16,224]{3,2,1,0:T(8,128)(2,1)} %bitcast.42), calls=%async_computation.5 | async-start | bytes 262144 | tf_op jit(solution)/shard_map/all_to_all | solution.py:72
  93.1 7.4 %copy-start.21 = (bf16[2,896,640]{2,1,0:T(8,128)(2,1)S(1)}, bf16[2,896,640]{2,1,0:T(8,128)(2,1)}, u32[]{:S(2)}) copy-start(bf16[2,896,640]{2,1,0:T(8,128)(2,1)} %param.28) | copy-start | bytes 6881284
  100.5 3.2 copy-start.4
  100.5 3.2 copy-start.23
  100.6 3.2 copy-start.24
  105.3 13.2 %all-to-all-start.3 = ((bf16[8,2,16,224]{3,2,1,0:T(8,128)(2,1)}), bf16[8,2,16,224]{3,2,1,0:T(8,128)(2,1)S(1)}, u32[]{:S(2)}, u32[]{:S(2)}) async-start(bf16[8,2,16,224]{3,2,1,0:T(8,128)(2,1)} %bitcast.20), calls=%async_computation.3 | async-start | bytes 262144 | tf_op jit(solution)/shard_map/all_to_all | solution.py:72
  111.0 39.8 %all-reduce.6.cloned.1.call-start = ((), (), s32[]{:S(2)}) async-start(), calls=%async_computation.11 | async-start | bytes 1835008 | tf_op jit(solution)/shard_map/psum | solution.py:128
  111.7 63.0 %reduce-scatter.4.cloned.1.call-start = ((), (), s32[]{:S(2)}) async-start(), calls=%async_computation.12 | async-start | bytes 573440 | tf_op jit(solution)/shard_map/reduce_scatter | solution.py:134
  131.1 98.1 %all-reduce.10.cloned.1.call-start = ((), (), s32[]{:S(2)}) async-start(), calls=%async_computation.16 | async-start | bytes 1835008 | tf_op jit(solution)/shard_map/psum | solution.py:173
  152.2 1.8 copy-start.13
  152.7 2.3 copy-start.16
  181.5 7.6 %copy-start.9 = (bf16[128,896]{1,0:T(8,128)(2,1)S(1)}, bf16[128,896]{1,0:T(8,128)(2,1)}, u32[]{:S(2)}) copy-start(bf16[128,896]{1,0:T(8,128)(2,1)} %param.27) | copy-start | bytes 688132
  181.5 7.9 %copy-start.17 = (bf16[256,128]{0,1:T(8,128)(2,1)S(1)}, bf16[256,128]{0,1:T(8,128)(2,1)}, u32[]{:S(2)}) copy-start(bf16[256,128]{0,1:T(8,128)(2,1)} %copy-done.16) | copy-start | bytes 196612
  182.7 7.0 %copy-start.5 = (bf16[256,224]{0,1:T(8,128)(2,1)}, bf16[256,224]{0,1:T(8,128)(2,1)S(1)}, u32[]{:S(2)}) copy-start(bf16[256,224]{0,1:T(8,128)(2,1)S(1)} %fusion.40) | copy-start | bytes 344068
  193.0 116.7 %all-reduce.8.cloned.1.call-start = ((), (), s32[]{:S(2)}) async-start(), calls=%async_computation.15 | async-start | bytes 1835008
  206.0 3.2 copy-start.22
  207.0 167.8 %reduce-scatter.8.cloned.1.call-start = ((), (), s32[]{:S(2)}) async-start(), calls=%async_computation.14 | async-start | bytes 516096 | tf_op jit(solution)/shard_map/reduce_scatter | solution.py:216
  209.1 230.9 %reduce-scatter.6.cloned.1.call-start = ((), (), s32[]{:S(2)}) async-start(), calls=%async_computation.13 | async-start | bytes 516096 | tf_op jit(solution)/shard_map/reduce_scatter | solution.py:212
  229.2 1.4 copy-start.3
  (7 other events, 6.0 us)
Sparse Core Ops, SparseCore 0:
  114.2 36.5 all-reduce.5
  153.4 21.3 reduce-scatter.3
  193.1 36.0 all-reduce.9
  232.5 77.0 all-reduce.7
  313.4 61.3 reduce-scatter.7
  378.5 61.5 reduce-scatter.5
